TPU v7x, 128 devices: a whole 4x4x4 slice. The times are simulated.
128 devices in a mesh: stream: 4 (over x), seq: 32 (over z, y, core).
Axes of the slice: x: 4, y: 4, z: 4, core: 2. Of those that a mesh axis runs over, the one named last changes fastest.
Arguments:
- conv_input: bfloat16 [4, 131072, 1280], P('stream', 'seq'), may hold values from -6 to 6
- conv_weight: float32 [4, 1280], replicated, may hold values from -3 to 3
- conv_bias: float32 [1280], replicated, may hold values from -1 to 1
- step_size: float32 [4, 16, 131072], P('stream', None, 'seq'), may hold values from 0.0005 to 0.005
- log_decay: float32 [4, 16, 131072], P('stream', None, 'seq'), as said below
- skip_gain: float32 [16], replicated, may hold values from 0.5 to 1.5
- doc_bounds: int32 [4, 128], P('stream'), may hold values from 1 to 131072, as said below
- doc_owner: int32 [4, 128], P('stream'), may hold values from 0 to 3, as said below
Outputs:
- mixed_out: bfloat16 [4, 131072, 1024], P('stream', 'seq')
- handoff_ssm: float32 [4, 32, 4, 2, 16, 64, 128], P('stream', 'seq')
- handoff_conv: bfloat16 [4, 32, 4, 2, 3, 1280], P('stream', 'seq')
Inputs may be any that keep to these rules, and one draw needn't show every extreme that they name: `doc_bounds`: each row rises and never falls; the real documents of a stream end at 131072, after which every entry equals 131072. At most 4 real documents have their last position in one run of 4096 positions starting at a multiple of 4096. `doc_owner`: among the real documents whose last positions lie in one such run of one stream, no owner is named more than 2 times. `log_decay`: never positive.
All inputs are finite; a program needn't handle non-finite values.
Results may differ from a plain program's by a relative error of at most 0.006.
Values may be sent and summed in bfloat16 or wider, within the bound.
A program may use at most 256 MiB of HBM per device.

v0:
```python
import jax
import jax.numpy as jnp
from jax import lax
from jax.sharding import PartitionSpec as P

P_SIZE = 64
N = 128
SPAN = 256
EMAX = 4
CAP = 2


def shifted(value, axis, steps):
    count = lax.axis_size(axis)
    leading, last = (max(0, -steps), min(count, count - steps))
    return lax.ppermute(value, axis, [(source, source + steps) for source in range(leading, last)])


def split_state(state):
    state_hi = state.astype(jnp.bfloat16)
    state_lo = (state - state_hi.astype(jnp.float32)).astype(jnp.bfloat16)
    return (state_hi, state_lo)


def span_output(
    x_span, b_span, c_span, dt_span, cum_decay, doc_span, prev_doc, state_in, skip_gain
):
    row_count = doc_span.shape[0]
    head_count = dt_span.shape[0]
    scores = jnp.einsum("tn,sn->ts", c_span, b_span, preferred_element_type=jnp.float32)
    position = jnp.arange(row_count)
    causal = (position[:, None] >= position[None, :]) & (doc_span[:, None] == doc_span[None, :])
    spread = cum_decay[:, :, None] - cum_decay[:, None, :]
    weights = jnp.where(
        causal[None],
        jnp.exp(jnp.where(causal[None], spread, 0.0)) * scores[None] * dt_span[:, None, :],
        0.0,
    ).astype(jnp.bfloat16)
    head_rows = x_span.reshape(row_count, head_count, -1)
    inner_part = jnp.einsum("hts,shp->thp", weights, head_rows, preferred_element_type=jnp.float32)
    entry_gate = jnp.where((doc_span == prev_doc)[None, :], jnp.exp(cum_decay), 0.0)
    state_hi, state_lo = split_state(state_in)
    outer_sum = jnp.einsum(
        "tn,hpn->thp", c_span, state_hi, preferred_element_type=jnp.float32
    ) + jnp.einsum("tn,hpn->thp", c_span, state_lo, preferred_element_type=jnp.float32)
    outer_part = outer_sum * entry_gate.T[:, :, None]
    summed = inner_part + outer_part + skip_gain[None, :, None] * head_rows.astype(jnp.float32)
    return summed.reshape(row_count, -1)


def carry_in(end_state, shard_gate, shard):
    head_count = shard_gate.shape[0]
    zeros_state = jnp.zeros(end_state.shape, jnp.float32)
    gates_all = lax.all_gather(shard_gate[None, :], "seq", axis=0, tiled=True)
    count = gates_all.shape[0]
    index_list = jnp.arange(count)
    before_me = (index_list < shard)[:, None]
    through = jnp.where(before_me, gates_all, 1.0)
    suffix = jnp.flip(jnp.cumprod(jnp.flip(through, 0), 0), 0)
    weights = jnp.where(
        before_me, jnp.concatenate([suffix[1:], jnp.ones((1, head_count), jnp.float32)], 0), 0.0
    )
    return zeros_state + jnp.sum(
        weights[:, :, None, None]
        * lax.all_gather(end_state[None].astype(jnp.bfloat16), "seq", axis=0, tiled=True).astype(
            jnp.float32
        ),
        0,
    )


def on_device(
    conv_input, conv_weight, conv_bias, step_size, log_decay, skip_gain, doc_bounds, doc_owner
):
    tok_count = conv_input.shape[1]
    head_count = step_size.shape[1]
    width = head_count * P_SIZE
    lag_rows = conv_weight.shape[0] - 1
    shard = lax.axis_index("seq")
    anchor = shard * tok_count
    rim_rows = shifted(conv_input[0, tok_count - lag_rows :], "seq", 1)
    padded = jnp.concatenate([rim_rows, conv_input[0]], 0)
    end_list = doc_bounds[0]
    owner_row = doc_owner[0]
    places = anchor - lag_rows + jnp.arange(tok_count + lag_rows, dtype=jnp.int32)
    docs_all = jnp.sum((end_list[None, :] <= places[:, None]).astype(jnp.int32), axis=1)
    own_doc = docs_all[lag_rows:]
    mixed_sum = conv_bias[None, :] + conv_weight[0][None, :] * conv_input[0].astype(jnp.float32)
    for lag_step in range(1, lag_rows + 1):
        moved_rows = padded[lag_rows - lag_step : lag_rows - lag_step + tok_count].astype(
            jnp.float32
        )
        same_doc = docs_all[lag_rows - lag_step : lag_rows - lag_step + tok_count] == own_doc
        mixed_sum = mixed_sum + conv_weight[lag_step][None, :] * jnp.where(
            same_doc[:, None], moved_rows, 0.0
        )
    activated = jax.nn.silu(mixed_sum).astype(jnp.bfloat16)
    count = tok_count // SPAN
    x_spans = activated[:, :width].reshape(count, SPAN, width)
    b_spans = activated[:, width : width + N].reshape(count, SPAN, N)
    c_spans = activated[:, width + N :].reshape(count, SPAN, N)
    dt_spans = step_size[0].reshape(head_count, count, SPAN).transpose(1, 0, 2)
    ld_spans = log_decay[0].reshape(head_count, count, SPAN).transpose(1, 0, 2)
    cum_spans = jnp.cumsum(ld_spans, axis=2)
    doc_spans = own_doc.reshape(count, SPAN)
    prev_docs = docs_all[lag_rows - 1 : lag_rows - 1 + tok_count : SPAN]
    end_weight = jnp.where(
        doc_spans[:, None, :] == doc_spans[:, None, -1:],
        jnp.exp(cum_spans[:, :, -1:] - cum_spans) * dt_spans,
        0.0,
    )
    loaded = (
        end_weight.transpose(0, 2, 1)[..., None]
        * x_spans.reshape(count, SPAN, head_count, P_SIZE).astype(jnp.float32)
    ).astype(jnp.bfloat16)
    block_states = jnp.einsum("cshp,csn->chpn", loaded, b_spans, preferred_element_type=jnp.float32)
    gates = jnp.where((doc_spans[:, -1] == prev_docs)[:, None], jnp.exp(cum_spans[:, :, -1]), 0.0)

    def advance(holding, item):
        block_state, gate = item
        return (block_state + gate[:, None, None] * holding, holding)

    end_state, hin_local = lax.scan(
        advance, jnp.zeros((head_count, P_SIZE, N), jnp.float32), (block_states, gates)
    )
    shard_gate = jnp.prod(gates, axis=0)
    lift = jnp.concatenate(
        [jnp.ones((1, head_count), jnp.float32), jnp.cumprod(gates, axis=0)[:-1]], 0
    )

    def span_rows(item):
        x_span, b_span, c_span, dt_span, cum_decay, doc_span, prev_doc, state_in = item
        return span_output(
            x_span, b_span, c_span, dt_span, cum_decay, doc_span, prev_doc, state_in, skip_gain
        )

    carried = carry_in(end_state, shard_gate, shard)
    hin_all = hin_local + lift[:, :, None, None] * carried
    out_rows = lax.map(
        span_rows, (x_spans, b_spans, c_spans, dt_spans, cum_spans, doc_spans, prev_docs, hin_all)
    ).astype(jnp.bfloat16)
    doc_index = jnp.arange(end_list.shape[0], dtype=jnp.int32)
    prior_end = jnp.concatenate([jnp.zeros((1,), jnp.int32), end_list[:-1]])
    real_docs = end_list > prior_end
    last_pos = jnp.clip(end_list - 1, 0, None)
    mine = real_docs & (last_pos >= anchor) & (last_pos < anchor + tok_count)
    earlier_doc = doc_index[None, :] < doc_index[:, None]
    owner_rank = jnp.sum(
        (mine[None, :] & (owner_row[None, :] == owner_row[:, None]) & earlier_doc).astype(
            jnp.int32
        ),
        axis=1,
    )
    order_rank = jnp.cumsum(mine.astype(jnp.int32)) - 1
    owner_count = lax.axis_size("stream")
    owner_ids = jnp.arange(owner_count)
    slot_ids = jnp.arange(CAP)
    ssm_send = jnp.zeros((owner_count, CAP, head_count, P_SIZE, N), jnp.float32)
    conv_send = jnp.zeros((owner_count, CAP, lag_rows, padded.shape[1]), jnp.bfloat16)
    for slot_index in range(EMAX):
        picked = mine & (order_rank == slot_index)
        valid = jnp.any(picked)
        doc_key = jnp.sum(jnp.where(picked, doc_index, 0))
        end_pos = jnp.sum(jnp.where(picked, end_list, 0))
        start_pos = jnp.sum(jnp.where(picked, prior_end, 0))
        target = jnp.sum(jnp.where(picked, owner_row, 0))
        slot_rank = jnp.sum(jnp.where(picked, owner_rank, 0))
        local_pos = jnp.clip(end_pos - 1 - anchor, 0, tok_count - 1)
        block = local_pos // SPAN
        offset = local_pos % SPAN
        x_span = lax.dynamic_index_in_dim(x_spans, block, 0, keepdims=False)
        b_span = lax.dynamic_index_in_dim(b_spans, block, 0, keepdims=False)
        dt_span = lax.dynamic_index_in_dim(dt_spans, block, 0, keepdims=False)
        cum_decay = lax.dynamic_index_in_dim(cum_spans, block, 0, keepdims=False)
        doc_span = lax.dynamic_index_in_dim(doc_spans, block, 0, keepdims=False)
        prev_doc = lax.dynamic_index_in_dim(prev_docs, block, 0, keepdims=False)
        state_in = lax.dynamic_index_in_dim(hin_all, block, 0, keepdims=False)
        kept_rows = (jnp.arange(SPAN) <= offset) & (doc_span == doc_key)
        scaled = jnp.where(
            kept_rows[None, :], jnp.exp(cum_decay[:, offset][:, None] - cum_decay) * dt_span, 0.0
        )
        slot_load = (
            scaled.T[:, :, None] * x_span.reshape(SPAN, head_count, P_SIZE).astype(jnp.float32)
        ).astype(jnp.bfloat16)
        final_state = jnp.einsum(
            "shp,sn->hpn", slot_load, b_span, preferred_element_type=jnp.float32
        )
        final_state = (
            final_state
            + jnp.where(prev_doc == doc_key, jnp.exp(cum_decay[:, offset]), 0.0)[:, None, None]
            * state_in
        )
        tail_rows = lax.dynamic_slice_in_dim(padded, local_pos + 1, lag_rows, 0)
        tail_pos = anchor + local_pos - (lag_rows - 1) + jnp.arange(lag_rows, dtype=jnp.int32)
        tail = jnp.where((tail_pos >= start_pos)[:, None], tail_rows, jnp.zeros_like(tail_rows))
        chosen = (owner_ids[:, None] == target) & (slot_ids[None, :] == slot_rank) & valid
        ssm_send = jnp.where(chosen[:, :, None, None, None], final_state[None, None], ssm_send)
        conv_send = jnp.where(chosen[:, :, None, None], tail[None, None], conv_send)
    got_ssm, got_conv = (
        lax.all_to_all(ssm_send, "stream", split_axis=0, concat_axis=0, tiled=True),
        lax.all_to_all(
            conv_send.astype(jnp.float32), "stream", split_axis=0, concat_axis=0, tiled=True
        ),
    )
    return (
        out_rows.reshape(1, tok_count, width),
        got_ssm[None, None],
        got_conv.astype(jnp.bfloat16)[None, None],
    )


def solution(mesh):
    in_specs = (
        P("stream", "seq", None),
        P(),
        P(),
        P("stream", None, "seq"),
        P("stream", None, "seq"),
        P(),
        P("stream", None),
        P("stream", None),
    )
    out_specs = (
        P("stream", "seq", None),
        P("stream", "seq", None, None, None, None, None),
        P("stream", "seq", None, None, None, None),
    )
    return jax.shard_map(
        on_device, mesh=mesh, in_specs=in_specs, out_specs=out_specs, check_vma=False
    )
```

profile of v0, /device:TPU:2, one launch (start us, length us, event | category | flops | bytes accessed | tf_op | source)
XLA Modules:
  0.0 458.2 jit_solution(13695956829510187057)
XLA Ops:
  7.9 1.7 collective-permute-start
  9.7 3.2 convert_reduce_fusion
  14.4 9.1 %reduce-window.19 = f32[16,16,2,128]{3,1,2,0:T(8,128)S(1)} reduce-window(f32[16,16,2,128]{3,1,2,0:T(8,128)S(1)} %copy_bitcast_fusion.1, f32[]{:T(128)} %constant.285.clone.1), window={size=1x1x1x128 pad=0_0x0_0x0_0x127_0}, to_apply=%region_1.2 | reduce-window | flops 8323072 | bytes 524292 | tf_op jit(solution)/shard_map/reduce-window
  27.1 31.0 %multiply_convert_fusion = bf16[4096,1280]{1,0:T(8,128)(2,1)S(1)} fusion(bf16[4096,1280]{1,0:T(8,128)(2,1)} %bitcast.256, bf16[3,1280]{1,0:T(4,128)(2,1)S(1)} %collective-permute-done, f32[1280]{0:T(1024)S(1)} %get-tuple-element.174, f32[1280]{0:T(1024)S(1)} %get-tuple-element.175, f32[1280]{0:T(1024)S(1)} %get-tuple-element.173, ...), kind=kLoop, calls=%fused_computation.51 | loop fusion | flops 152043520 | bytes 21017088 | tf_op jit(solution)/shard_map/convert_element_type | solution.py:97
  58.1 9.1 %slice_convert_fusion = (f32[4096,1024]{1,0:T(8,128)}, bf16[4096,1024]{1,0:T(8,128)(2,1)}) fusion(bf16[4096,1280]{1,0:T(8,128)(2,1)S(1)} %multiply_convert_fusion), kind=kLoop, calls=%fused_computation.224 | loop fusion | flops 4194304 | bytes 33554432 | tf_op jit(solution)/shard_map/convert_element_type | solution.py:114
  68.3 17.5 %copy.97 = f32[4096,1024]{0,1:T(8,128)} copy(f32[4096,1024]{1,0:T(8,128)} %get-tuple-element.250) | data formatting | bytes 33554432 | tf_op jit(solution)/shard_map/convert_element_type | solution.py:114
  85.8 11.0 %copy.123 = f32[128,8,16,256]{3,2,1,0:T(8,128)S(1)} copy(f32[128,8,16,256]{3,1,2,0:T(8,128)} %bitcast.252) | data formatting | bytes 33554432
  96.8 2.4 multiply_convert_fusion.1
  99.2 6.2 %fusion.34 = f32[16,16,64,128]{3,2,1,0:T(8,128)} fusion(bf16[16,256,128,1]{2,1,3,0:T(8,128)(2,1)S(1)} %bitcast.260, bf16[16,256,16,64]{1,0,3,2:T(8,128)(2,1)S(1)} %multiply_convert_fusion.1), kind=kOutput, calls=%fused_computation.62 | convolution fusion | flops 1073741824 | bytes 17825792 | tf_op jit(solution)/shard_map/cshp,csn->chpn/dot_general | solution.py:116
  105.4 32.6 %while.24 = (s32[]{:T(128)}, f32[16,64,128]{2,1,0:T(8,128)S(1)}, f32[16,16,64,128]{3,2,1,0:T(8,128)}, f32[16,16,64,128]{3,2,1,0:T(8,128)}, f32[16,16]{1,0:T(8,128)S(1)}, /*index=5*/s32[]{:T(128)}, s32[]{:T(128)}) while((s32[]{:T(128)}, f32[16,64,128]{2,1,0:T(8,128)S(1)}, f32[16,16,64,128]{3,2,1,0:T(8,128)}, ...), condition=%wide.region_4.5_spmd.clone, body=%wide.region_3.4_spmd.clone.sunk | while | flops 524291 | bytes 2622240 | solution.py:123
  150.3 2.5 and_reduce_fusion.3
  154.4 1.6 copy.107
  157.0 2.6 copy.109
  160.7 2.6 copy.111
  164.7 68.9 %all-reduce.2 = f32[512]{0:T(512)S(1)} all-reduce(f32[512]{0:T(512)S(1)} %dynamic-update-slice), channel_id=2, replica_groups=mesh['stream'=4,'seq'=32] {'seq'}, use_global_device_ids=true, to_apply=%add.2 | all-reduce | flops 512 | bytes 4096
  248.5 4.8 %all-to-all-start.1 = ((bf16[4,2,3,1280]{3,1,2,0:T(2,128)(2,1)}), bf16[4,2,3,1280]{3,1,2,0:T(2,128)(2,1)S(1)}, u32[]{:S(2)}, u32[]{:S(2)}) async-start(bf16[4,2,3,1280]{3,1,2,0:T(2,128)(2,1)} %fusion.45), calls=%async_computation.1 | async-start | bytes 122880 | tf_op jit(solution)/shard_map/all_to_all | solution.py:201
  253.3 4.1 multiply_convert_fusion.5
  262.4 5.1 %fusion.30 = f32[16,64,128]{2,1,0:T(8,128)S(1)} fusion(bf16[32,16,64,128]{3,2,1,0:T(8,128)(2,1)} %bitcast.266, f32[32,16]{1,0:T(8,128)S(1)} %pad_select_fusion), kind=kLoop, calls=%fused_computation.53 | loop fusion | flops 12451840 | bytes 8914944 | tf_op jit(solution)/shard_map/reduce_sum | solution.py:63
  267.5 4.1 multiply_add_fusion
  272.6 2.3 copy-done
  275.2 3.2 select_select_fusion
  278.4 5.1 %all-to-all-start = ((f32[4,2,16,64,128]{4,3,2,1,0:T(8,128)}), f32[4,2,16,64,128]{4,3,2,1,0:T(8,128)}, u32[]{:S(2)}, u32[]{:S(2)}) async-start(f32[4,2,16,64,128]{4,3,2,1,0:T(8,128)} %select_select_fusion), calls=%async_computation | async-start | bytes 8388608 | tf_op jit(solution)/shard_map/all_to_all | solution.py:200
  283.6 150.2 %while.23 = (s32[]{:T(128)}, bf16[16,256,1024]{1,2,0:T(8,128)(2,1)}, bf16[16,256,1024]{2,1,0:T(8,128)(2,1)}, s32[16,256]{1,0:T(8,128)S(1)}, f32[16,16,256]{2,1,0...) while((s32[]{:T(128)}, ...), condition=%wide.region_10.11_spmd, body=%wide.region_9.10_spmd.sunk | while | flops 294064384 | bytes 10755285 | solution.py:139
  309.5 1.4 fusion.109
  365.8 1.4 fusion.109
  375.1 1.4 fusion.109
  384.6 1.4 fusion.109
  393.9 1.4 fusion.109
  403.3 1.4 fusion.109
  431.4 1.4 fusion.109
  433.7 12.2 %copy.100 = bf16[16,256,1024]{2,1,0:T(8,128)(2,1)} copy(bf16[16,256,1024]{1,2,0:T(8,128)(2,1)} %get-tuple-element.90) | data formatting | bytes 16777216 | tf_op jit(solution)/shard_map/convert_element_type | solution.py:141
  445.9 4.8 %copy.163 = f32[1,1,4,2,16,64,128]{6,5,4,3,2,1,0:T(8,128)} copy(f32[1,1,4,2,16,64,128]{6,5,4,3,2,1,0:T(8,128)} %bitcast.66) | data formatting | bytes 8388608
  (336 shorter events, 209.1 us)
Async XLA Ops:
  7.2 255.2 %all-gather.4.cloned.1.call-start = ((), (), s32[]{:S(2)}) async-start(), calls=%async_computation.2 | async-start | bytes 8650752 | tf_op jit(solution)/shard_map/all_gather | solution.py:65
  7.9 19.2 %collective-permute-start = (bf16[3,1280]{1,0:T(4,128)(2,1)S(1)}, bf16[3,1280]{1,0:T(4,128)(2,1)S(1)}, u32[]{:S(2)}, u32[]{:S(2)}) collective-permute-start(bf16[3,1280]{1,0:T(4,128)(2,1)S(1)} %slice_bitcast_fusion), channel_id=1, source_target_pairs={{0,1},{1,2},{2,3},{3,4},{4,5},{5,6},{6,7},{7,8},{8,9},{9,10},{10,1... | collective-permute-start | bytes 23048 | tf_op jit(solution)/shard_map/ppermute | solution.py:16
  105.4 33.4 %copy-start.1 = (s32[1,128]{1,0:T(1,128)S(1)}, s32[1,128]{1,0:T(1,128)}, u32[]{:S(2)}) copy-start(s32[1,128]{1,0:T(1,128)} %param.18) | copy-start | bytes 1540
  105.4 34.0 %copy-start.3 = (s32[1,128]{1,0:T(1,128)S(1)}, s32[1,128]{1,0:T(1,128)}, u32[]{:S(2)}) copy-start(s32[1,128]{1,0:T(1,128)} %param.19) | copy-start | bytes 1540
  138.0 25.2 %copy-start.4 = (u32[128]{0:T(128)S(1)}, u32[128]{0:T(128)}, u32[]{:S(2)}) copy-start(u32[128]{0:T(128)} %constant.317) | copy-start | bytes 1540
  248.5 13.9 %all-to-all-start.1 = ((bf16[4,2,3,1280]{3,1,2,0:T(2,128)(2,1)}), bf16[4,2,3,1280]{3,1,2,0:T(2,128)(2,1)S(1)}, u32[]{:S(2)}, u32[]{:S(2)}) async-start(bf16[4,2,3,1280]{3,1,2,0:T(2,128)(2,1)} %fusion.45), calls=%async_computation.1 | async-start | bytes 122880 | tf_op jit(solution)/shard_map/all_to_all | solution.py:201
  271.7 3.2 copy-start
  272.6 10.9 %copy-start.2 = (f32[16]{0:T(128)S(1)}, f32[16]{0:T(128)}, u32[]{:S(2)}) copy-start(f32[16]{0:T(128)} %param.17) | copy-start | bytes 196
  278.4 167.5 %all-to-all-start = ((f32[4,2,16,64,128]{4,3,2,1,0:T(8,128)}), f32[4,2,16,64,128]{4,3,2,1,0:T(8,128)}, u32[]{:S(2)}, u32[]{:S(2)}) async-start(f32[4,2,16,64,128]{4,3,2,1,0:T(8,128)} %select_select_fusion), calls=%async_computation | async-start | bytes 8388608 | tf_op jit(solution)/shard_map/all_to_all | solution.py:200
Sparse Core Ops, SparseCore 0:
  138.9 56.7 all-gather.3
where the time goes:
time: 464 us; the launch traced here: 458 us
  other arithmetic  137 us (30%)
  local copies, waits for them, and re-layouts  128 us (28%)
  matrix products  89.1 us (19%)
  blocking collectives  68.9 us (15%)
  between operations  22.7 us (5%)
  starting transfers between devices  11.7 us (3%)
    unnamed x1, blocking collectives  68.9 us
    convert_element_type x1, other arithmetic, on_device(): activated = jax.nn.silu(mixed_sum).astype(jnp.bfloat16)  31 us
    dynamic_slice x48, local copies, waits for them, and re-layouts, on_device(): lax.map(span_rows, (x_spans, b_spans, c_spans, dt_spans, cum_spans, doc_s...  29.9 us
    dot_general x16, matrix products, span_output(): jnp.einsum('tn,hpn->thp', c_span, state_lo, preferred_element_type=jnp.fl...  23.1 us
    dot_general x16, matrix products, span_output(): jnp.einsum('tn,hpn->thp', c_span, state_hi, preferred_element_type=jnp.fl...  22 us
    unnamed x18, local copies, waits for them, and re-layouts  21.6 us
    dot_general x16, matrix products, span_output(): jnp.einsum('hts,shp->thp', weights, head_rows, preferred_element_type=jnp...  20.2 us
    add x16, other arithmetic, advance(): return (block_state + gate[:, None, None] * holding, holding)  18.5 us
  transfers between devices with their start and end apart: 4, of which 0 were waited for; matrix products, arithmetic and copies ran while one was open for 48% of the time, Pallas kernels for 0%

commit v1 on v0

v1 whole, which is shorter than its diff:
```python
import functools

import jax
import jax.numpy as jnp
from jax import lax
from jax.experimental import pallas as pl
from jax.experimental.pallas import tpu as pltpu
from jax.sharding import PartitionSpec as P

MESH = pl.DeviceIdType.MESH
F32 = jnp.float32
BF16 = jnp.bfloat16
T = 4096
CH = 1280
W = 1024
H = 16
N = 128
L = 64
BLK = 256
STEPS = T // BLK
NC = T // L
NSEQ = 32
NSTR = 4
PAY = 1056
BIG = 1 << 20
LOG2E = 1.4426950408889634


def dot(a, b, ca=1, cb=0):
    return lax.dot_general(a, b, (((ca,), (cb,)), ((), ())), preferred_element_type=F32)


def iota(shape, dim):
    return lax.broadcasted_iota(jnp.int32, shape, dim)


def doc_start(pos, meta):
    start = jnp.full(pos.shape, meta[13], jnp.int32)
    for n in range(4):
        start = jnp.where(pos >= meta[n], meta[n], start)
    return start


def doc_end(pos, meta):
    end = jnp.full(pos.shape, T, jnp.int32)
    for n in range(3, -1, -1):
        end = jnp.where(pos < meta[n], jnp.minimum(meta[n], T), end)
    return end


def pick(table, lane):
    return jnp.take_along_axis(table, lane, axis=1)


def left(v, s):
    return pltpu.roll(v, v.shape[1] - s, 1)


def scan_docs(bounds, owners, meta, anchor):
    for k in range(16):
        meta[k] = BIG if k < 4 else 0
    meta[13] = -anchor

    def body(k, prev):
        bound = bounds[k]

        @pl.when((bound <= anchor) & (bound > prev))
        def _():
            meta[13] = bound - anchor

        @pl.when((bound > anchor) & (bound <= anchor + T) & (bound > prev))
        def _():
            n = meta[12]
            owner = owners[k]
            rank = jnp.int32(0)
            for m in range(4):
                same = (m < n) & (meta[4 + m] == owner)
                rank = rank + jnp.where(same, 1, 0).astype(jnp.int32)
            meta[n] = bound - anchor
            meta[4 + n] = owner
            meta[8 + n] = rank
            meta[12] = n + 1

        return bound

    lax.fori_loop(0, bounds.shape[0], body, jnp.int32(0))


def decay_tables(meta, ld, dt, ldr, dtr, cols, crow, grow, gate, wide, table):
    pos = iota((1, T), 1)
    end = doc_end(pos, meta)
    wide[0:1, :] = doc_start(pos, meta)
    wide[1:2, :] = end
    for half in range(2):
        heads = slice(8 * half, 8 * half + 8)
        v = ld[heads, :] * LOG2E
        seg = jnp.where(pos + 1 < end, left(v, 1), 0.0)
        for k in range(12):
            s = 1 << k
            seg = seg + jnp.where(pos + s < end, left(seg, s), 0.0)
        whole = jnp.exp2(v[:, :1] + seg[:, :1])
        gate[heads, :] = jnp.broadcast_to(jnp.where(meta[13] < 0, whole, 0.0), (8, N))
        table[48 + 8 * half : 56 + 8 * half, :] = jnp.exp2(seg) * dt[heads, :]
    table[64:N, :] = jnp.zeros((N - 64, T), F32)

    def narrow(b, _):
        at = pl.ds(pl.multiple_of(b * N, N), N)
        place = iota((1, N), 1)
        base = b * N + place - place % L
        start = wide[0:1, at]
        end = wide[1:2, at]
        v = ld[:, at] * LOG2E
        cum = v
        suf = jnp.where(place % L + 1 < L, left(v, 1), 0.0)
        for k in range(6):
            s = 1 << k
            cum = cum + jnp.where(place % L >= s, pltpu.roll(cum, s, 1), 0.0)
            suf = suf + jnp.where(place % L + s < L, left(suf, s), 0.0)
        table[0:H, at] = cum
        table[H : 2 * H, at] = jnp.where(end >= base + L, jnp.exp2(suf) * dt[:, at], 0.0)
        table[2 * H : 3 * H, at] = jnp.where(start < base, jnp.exp2(cum), 0.0)
        cols[at, :] = table[:, at].T
        return 0

    lax.fori_loop(0, T // N, narrow, 0, unroll=4)
    first = iota((NC, 1), 0) * L
    open_block = doc_start(first + (L - 1), meta) < first
    lane = iota((NC, N), 1) % L
    for j in range(8):
        lanes = slice(j * N, (j + 1) * N)
        v = ldr[:, lanes] * LOG2E
        cum = v
        suf = jnp.where(lane + 1 < L, left(v, 1), 0.0)
        for k in range(6):
            s = 1 << k
            cum = cum + jnp.where(lane >= s, pltpu.roll(cum, s, 1), 0.0)
            suf = suf + jnp.where(lane + s < L, left(suf, s), 0.0)
        crow[j] = cum - jnp.log2(dtr[:, lanes])
        grow[j] = jnp.where(open_block, jnp.exp2(cum + suf), 0.0)


def first_kernel(
    bounds, owners, x_ref, halo, cw, cb, ld, dt, ldr, dtr,
    act, cols, crow, grow, gate, ends, sends, meta,
    xf, acc, half, wide, table, load,
):
    i = pl.program_id(0)
    anchor = lax.axis_index("seq") * T

    @pl.when(i == 0)
    def _():
        scan_docs(bounds, owners, meta, anchor)
        decay_tables(meta, ld, dt, ldr, dtr, cols, crow, grow, gate, wide, table)
        acc[...] = jnp.zeros_like(acc)
        sends[...] = jnp.zeros_like(sends)
        half[0:4, :] = cw[...] * 0.5
        half[4:5, :] = cb[...] * 0.5
        before = iota((16, 1), 0) - 16
        real = (before >= meta[13]) & (anchor > 0)
        for j in range(CH // N):
            rows = halo[:, j * N : (j + 1) * N].astype(F32)
            xf[j, 0:16, :] = jnp.where(real, rows, 0.0)

    for j in range(CH // N):
        lanes = slice(j * N, (j + 1) * N)
        xf[j, 16 : 16 + BLK, :] = x_ref[:, lanes].astype(F32)
        for r in range(0, BLK, 64):
            v = half[4:5, lanes] + half[0:1, lanes] * xf[j, 16 + r : 80 + r, :]
            for k in range(1, 4):
                v = v + half[k : k + 1, lanes] * xf[j, 16 + r - k : 80 + r - k, :]
            act[r : r + 64, lanes] = (v + v * jnp.tanh(v)).astype(BF16)

    def fix(m, _):
        doc_begin = meta[m >> 1]
        group = (doc_begin + 2 * (m & 1)) >> 4
        again = ((m & 1) == 1) & (group == doc_begin >> 4)

        @pl.when((group >> 4 == i) & jnp.logical_not(again))
        def _():
            at = pl.multiple_of((group & 15) * 16, 16)
            pos = group * 16 + iota((16, 1), 0)
            start = doc_start(pos, meta)
            for j in range(CH // N):
                lanes = slice(j * N, (j + 1) * N)
                rows = xf[j, pl.ds(at, 32), :]
                v = half[4:5, lanes] + half[0:1, lanes] * rows[16:32]
                for k in range(1, 4):
                    moved = jnp.where(pos - k >= start, rows[16 - k : 32 - k], 0.0)
                    v = v + half[k : k + 1, lanes] * moved
                act[pl.ds(at, 16), lanes] = (v + v * jnp.tanh(v)).astype(BF16)

        return 0

    touched = jnp.bool_(False)
    for n in range(4):
        touched = touched | ((meta[n] - 1) >> 8 == i) | ((meta[n] + 2) >> 8 == i)

    @pl.when(touched)
    def _():
        lax.fori_loop(0, 8, fix, 0)

    def take_tail(n, _):
        last = meta[n] - 1

        @pl.when(last >> 8 == i)
        def _():
            row = iota((32, 16 + BLK), 0)
            at = iota((32, 16 + BLK), 1) - 16 + i * BLK
            begin = jnp.where(n > 0, meta[jnp.maximum(n - 1, 0)], meta[13])
            total = jnp.zeros((32, N), F32)
            for j in range(CH // N):
                lag = row - 3 * j
                hit = (lag >= 0) & (lag < 3) & (at == last - 2 + lag) & (at >= begin)
                total = total + dot(jnp.where(hit, 1.0, 0.0).astype(BF16), xf[j].astype(BF16))
            sends[meta[8 + n], meta[4 + n], W:PAY, :] = total.astype(BF16)

        return 0

    @pl.when(touched)
    def _():
        lax.fori_loop(0, 4, take_tail, 0)

    for j in range(CH // N):
        xf[j, 0:16, :] = xf[j, BLK : BLK + 16, :]

    part = iota((L, N), 1) // L
    for r in range(0, BLK, L):
        col = cols[pl.ds(pl.multiple_of(i * BLK + r, L), L), :]
        for j in range(8):
            lanes = slice(j * N, (j + 1) * N)
            weight = pick(col, part + (2 * j + 3 * H)).astype(BF16)
            load[r : r + L, lanes] = act[r : r + L, lanes] * weight
    low = jnp.int32(0)
    high = jnp.int32(0)
    for n in range(4):
        low = low + jnp.where(meta[n] <= i * BLK, 1, 0).astype(jnp.int32)
        high = high + jnp.where(meta[n] <= i * BLK + BLK - 1, 1, 0).astype(jnp.int32)
    row = i * BLK + iota((BLK, 1), 0)

    def segment(j, _):
        begin = jnp.where(j > 0, meta[jnp.maximum(j - 1, 0)], 0)
        stop = jnp.where(j < 4, meta[jnp.minimum(j, 3)], BIG)
        kept = jnp.where((row >= begin) & (row < stop), act[:, W : W + N].astype(F32), 0.0)
        flipped = kept.astype(BF16).T
        for g in range(4):
            wide_lanes = slice(g * 2 * N, (g + 1) * 2 * N)
            acc[j, :, wide_lanes] = acc[j, :, wide_lanes] + dot(flipped, load[:, wide_lanes])
        return 0

    lax.fori_loop(low, high + 1, segment, 0)

    @pl.when(i == STEPS - 1)
    def _():
        for b in range(8):
            tile = acc[meta[12], :, b * N : (b + 1) * N].T
            ends[b * N : (b + 1) * N, :] = tile.astype(BF16)

        def put(n, _):
            for b in range(8):
                tile = acc[n, :, b * N : (b + 1) * N].T
                sends[meta[8 + n], meta[4 + n], b * N : (b + 1) * N, :] = tile.astype(BF16)
            return 0

        lax.fori_loop(0, meta[12], put, 0)


def run_first(bounds, owners, x, halo, cw, cb, ld, dt, ldr, dtr):
    smem = pl.BlockSpec(memory_space=pltpu.SMEM)
    full = lambda *shape: pl.BlockSpec(shape, lambda i: (0,) * len(shape))
    return pl.pallas_call(
        first_kernel,
        grid=(STEPS,),
        in_specs=[
            smem, smem, pl.BlockSpec((BLK, CH), lambda i: (i, 0)), full(16, CH), full(4, CH),
            full(1, CH), full(H, T), full(H, T), full(NC, W), full(NC, W),
        ],
        out_specs=[
            pl.BlockSpec((BLK, CH), lambda i: (i, 0)), full(T, N), full(8, NC, N), full(8, NC, N),
            full(H, N), full(W, N), full(2, NSTR, PAY, N), smem,
        ],
        out_shape=[
            jax.ShapeDtypeStruct((T, CH), BF16), jax.ShapeDtypeStruct((T, N), F32),
            jax.ShapeDtypeStruct((8, NC, N), F32), jax.ShapeDtypeStruct((8, NC, N), F32),
            jax.ShapeDtypeStruct((H, N), F32), jax.ShapeDtypeStruct((W, N), BF16),
            jax.ShapeDtypeStruct((2, NSTR, PAY, N), BF16), jax.ShapeDtypeStruct((16,), jnp.int32),
        ],
        scratch_shapes=[
            pltpu.VMEM((CH // N, BLK + 16, N), F32), pltpu.VMEM((5, N, W), F32),
            pltpu.VMEM((8, CH), F32), pltpu.VMEM((8, T), jnp.int32), pltpu.VMEM((N, T), F32),
            pltpu.VMEM((BLK, W), BF16),
        ],
        compiler_params=pltpu.CompilerParams(dimension_semantics=("arbitrary",)),
        name="first",
    )(bounds, owners, x, halo, cw, cb, ld, dt, ldr, dtr)


def exchange_kernel(
    meta, ends, gate, sends, carried, got,
    seen, seen_gate, prefix, fixed, my_gate,
    s1, r1, s2, r2, s3, r3, s4, r4, own_sem,
):
    me = lax.axis_index("seq")
    st = lax.axis_index("stream")
    barrier = pltpu.get_barrier_semaphore()

    @pl.loop(1, NSEQ)
    def _(k):
        pl.semaphore_signal(
            barrier, inc=1, device_id=(st, lax.rem(me + k, NSEQ)), device_id_type=MESH
        )

    for k in range(1, NSTR):
        pl.semaphore_signal(
            barrier, inc=1, device_id=(lax.rem(st + k, NSTR), me), device_id_type=MESH
        )
    my_gate[...] = jnp.where(meta[12] == 0, gate[...], 0.0)
    pl.semaphore_wait(barrier, NSEQ - 1 + NSTR - 1)

    def handoff(k, slot, src, s, r):
        to = lax.rem(st + k, NSTR)
        return pltpu.make_async_remote_copy(
            src_ref=src.at[to], dst_ref=got.at[slot, st], send_sem=s.at[k], recv_sem=r.at[k],
            device_id=(to, me), device_id_type=MESH,
        )

    def spread(k):
        to = lax.rem(me + k, NSEQ)
        state = pltpu.make_async_remote_copy(
            src_ref=ends.at[to], dst_ref=seen.at[me], send_sem=s1.at[k], recv_sem=r1.at[k],
            device_id=(st, to), device_id_type=MESH,
        )
        factor = pltpu.make_async_remote_copy(
            src_ref=my_gate.at[pl.ds(lax.div(to, 2), 1)], dst_ref=seen_gate.at[pl.ds(me, 1)],
            send_sem=s2.at[k], recv_sem=r2.at[k], device_id=(st, to), device_id_type=MESH,
        )
        return state, factor

    def give(k):
        to = lax.rem(me + k, NSEQ)
        return pltpu.make_async_remote_copy(
            src_ref=prefix.at[to], dst_ref=carried.at[me], send_sem=s1.at[NSEQ + k],
            recv_sem=r1.at[NSEQ + k], device_id=(st, to), device_id_type=MESH,
        )

    for k in range(1, NSEQ):
        state, factor = spread(k)
        factor.start()
        state.start()
    for k in range(1, NSTR):
        handoff(k, 1, sends.at[1], s3, r3).start()
    own = pltpu.make_async_copy(sends.at[1, st], got.at[1, st], own_sem)
    own.start()
    seen[pl.ds(me, 1)] = ends[pl.ds(me, 1)]
    seen_gate[pl.ds(me, 1), :] = my_gate[pl.ds(lax.div(me, 2), 1), :]
    for k in range(1, NSEQ):
        state, factor = spread(k)
        factor.wait()
        state.wait()

    def step(q, state):
        prefix[q] = state.astype(BF16)
        return seen[q].astype(F32) + seen_gate[pl.ds(q, 1), :] * state

    lax.fori_loop(0, NSEQ, step, jnp.zeros((32, N), F32))
    for k in range(1, NSEQ):
        give(k).start()
    carried[pl.ds(me, 1)] = prefix[pl.ds(me, 1)]
    for k in range(1, NSEQ):
        give(k).wait()

    def correct(d, _):
        lift = jnp.where(meta[12] > 0, gate[pl.ds(lax.div(d, 2), 1), :], 0.0)
        extra = carried[d].astype(F32) * lift
        rows = pl.ds(pl.multiple_of(d * 32, 32), 32)
        for o in range(NSTR):
            mine = jnp.where(meta[4] == o, extra, 0.0)
            fixed[o, rows, :] = (sends[0, o, rows, :].astype(F32) + mine).astype(BF16)
        return 0

    lax.fori_loop(0, NSEQ, correct, 0)
    for o in range(NSTR):
        fixed[o, W:PAY, :] = sends[0, o, W:PAY, :]
    for k in range(1, NSTR):
        handoff(k, 0, fixed, s4, r4).start()
    own.wait()
    got[pl.ds(0, 1), pl.ds(st, 1)] = fixed[pl.ds(st, 1)][None]
    for k in range(1, NSTR):
        handoff(k, 1, sends.at[1], s3, r3).wait()
        handoff(k, 0, fixed, s4, r4).wait()


def run_exchange(meta, ends, gate, sends):
    vmem = pl.BlockSpec(memory_space=pltpu.VMEM)
    dma = pltpu.SemaphoreType.DMA
    return pl.pallas_call(
        exchange_kernel,
        in_specs=[pl.BlockSpec(memory_space=pltpu.SMEM), vmem, vmem, vmem],
        out_specs=[vmem, vmem],
        out_shape=[
            jax.ShapeDtypeStruct((NSEQ, 32, N), BF16),
            jax.ShapeDtypeStruct((2, NSTR, PAY, N), BF16),
        ],
        scratch_shapes=[
            pltpu.VMEM((NSEQ, 32, N), BF16), pltpu.VMEM((NSEQ, N), F32),
            pltpu.VMEM((NSEQ, 32, N), BF16), pltpu.VMEM((NSTR, PAY, N), BF16),
            pltpu.VMEM((H, N), F32),
            dma((2 * NSEQ,)), dma((2 * NSEQ,)), dma((NSEQ,)), dma((NSEQ,)),
            dma((NSTR,)), dma((NSTR,)), dma((NSTR,)), dma((NSTR,)), dma,
        ],
        compiler_params=pltpu.CompilerParams(collective_id=0, has_side_effects=True),
        name="exchange",
    )(meta, ends, gate, sends)


def last_kernel(
    meta, skip, act, cols, crow, grow, carried, got,
    out, ssm, tails,
    h, hb, skips,
):
    i = pl.program_id(0)

    @pl.when(i == 0)
    def _():
        lane = iota((L, N), 1)
        for j in range(8):
            gain = jnp.where(lane < L, skip[2 * j], skip[2 * j + 1])
            skips[j] = jnp.where(lane % L == iota((L, N), 0), gain, 0.0).astype(BF16)
            tile = carried[j * N : (j + 1) * N, :].astype(F32).T
            h[:, j * N : (j + 1) * N] = tile
            hb[:, j * N : (j + 1) * N] = tile.astype(BF16)

    @pl.when(i < 8)
    def _():
        ssm[...] = got[0, 0, 0:W, :].astype(F32).reshape(ssm.shape)
        tail = got[0, 0, W:PAY, :].astype(F32)
        for j in range(CH // N):
            for k in range(3):
                row = tail[3 * j + k : 3 * j + k + 1, :].astype(BF16)
                tails[0, 0, k : k + 1, j * N : (j + 1) * N] = row

    part = iota((L, N), 1) // L
    zero = jnp.zeros((L, N), BF16)
    for q in range(BLK // L):
        rows = slice(q * L, (q + 1) * L)
        c = i * (BLK // L) + q
        cmat = act[rows, W + N : CH]
        bmat = act[rows, W : W + N]
        flipped = bmat.T
        col = cols[rows, :]
        score = dot(cmat, jnp.concatenate([bmat, bmat], 0), 1, 1)
        pos = c * L + iota((L, N), 0)
        src = c * L + iota((L, N), 1) % L
        keep = (src <= pos) & (src >= doc_start(pos, meta))
        score = jnp.where(keep, score, 0.0).astype(BF16)
        for g in range(4):
            wide = slice(g * 2 * N, (g + 1) * 2 * N)
            mix, pairs, entry, loads = [], [], [], []
            for j in (2 * g, 2 * g + 1):
                x = act[rows, j * N : (j + 1) * N]
                spread = pick(col, part + 2 * j) - crow[j, pl.ds(c, 1), :]
                mix.append(jnp.exp2(jnp.minimum(spread, 30.0)).astype(BF16) * score + skips[j])
                for half in (0, 1):
                    own = jnp.where(part == half, x, zero)
                    pairs.append(jnp.concatenate([own, zero] if j == 2 * g else [zero, own], 1))
                loads.append(x * pick(col, part + (2 * j + H)).astype(BF16))
                entry.append(pick(col, part + (2 * j + 2 * H)))
            inner = dot(jnp.concatenate(mix, 1), jnp.concatenate(pairs, 0))
            outer = dot(cmat, hb[:, wide]) * jnp.concatenate(entry, 1)
            out[rows, wide] = (inner + outer).astype(BF16)
            fresh = dot(flipped, jnp.concatenate(loads, 1))
            for j in (0, 1):
                lanes = slice((2 * g + j) * N, (2 * g + j + 1) * N)
                state = grow[2 * g + j, pl.ds(c, 1), :] * h[:, lanes] + fresh[:, j * N : (j + 1) * N]
                h[:, lanes] = state
                hb[:, lanes] = state.astype(BF16)


def run_last(meta, skip, act, cols, crow, grow, carried, got):
    smem = pl.BlockSpec(memory_space=pltpu.SMEM)
    full = lambda *shape: pl.BlockSpec(shape, lambda i: (0,) * len(shape))
    slot = lambda i: jnp.minimum(i, 7)
    return pl.pallas_call(
        last_kernel,
        grid=(STEPS,),
        in_specs=[
            smem, smem, pl.BlockSpec((BLK, CH), lambda i: (i, 0)),
            pl.BlockSpec((BLK, N), lambda i: (i, 0)), full(8, NC, N), full(8, NC, N), full(W, N),
            pl.BlockSpec((1, 1, PAY, N), lambda i: (slot(i) % 2, slot(i) // 2, 0, 0)),
        ],
        out_specs=[
            pl.BlockSpec((BLK, W), lambda i: (i, 0)),
            pl.BlockSpec((1, 1, H, L, N), lambda i: (slot(i) // 2, slot(i) % 2, 0, 0, 0)),
            pl.BlockSpec((1, 1, 3, CH), lambda i: (slot(i) // 2, slot(i) % 2, 0, 0)),
        ],
        out_shape=[
            jax.ShapeDtypeStruct((T, W), BF16),
            jax.ShapeDtypeStruct((NSTR, 2, H, L, N), F32),
            jax.ShapeDtypeStruct((NSTR, 2, 3, CH), BF16),
        ],
        scratch_shapes=[
            pltpu.VMEM((N, W), F32), pltpu.VMEM((N, W), BF16), pltpu.VMEM((8, L, N), BF16),
        ],
        compiler_params=pltpu.CompilerParams(dimension_semantics=("arbitrary",)),
        name="last",
    )(meta, skip, act, cols, crow, grow, carried, got)


def by_block(rows):
    return rows.reshape(H, NC, L).transpose(1, 0, 2).reshape(NC, W)


def on_device(x, cw, cb, dt, ld, skip, bounds, owners):
    x, dt, ld = x[0], dt[0], ld[0]
    halo = lax.ppermute(x[T - 16 :], "seq", [(k, k + 1) for k in range(NSEQ - 1)])
    act, cols, crow, grow, gate, ends, sends, meta = run_first(
        bounds[0], owners[0], x, halo, cw, cb[None], ld, dt, by_block(ld), by_block(dt)
    )
    carried, got = run_exchange(meta, ends.reshape(NSEQ, 32, N), gate, sends)
    out, ssm, tails = run_last(
        meta, skip, act, cols, crow, grow, carried.reshape(W, N), got
    )
    return out[None], ssm[None, None], tails[None, None]


def solution(mesh):
    in_specs = (
        P("stream", "seq", None),
        P(),
        P(),
        P("stream", None, "seq"),
        P("stream", None, "seq"),
        P(),
        P("stream", None),
        P("stream", None),
    )
    out_specs = (
        P("stream", "seq", None),
        P("stream", "seq", None, None, None, None, None),
        P("stream", "seq", None, None, None, None),
    )
    return jax.shard_map(
        on_device, mesh=mesh, in_specs=in_specs, out_specs=out_specs, check_vma=False
    )
```

time: 464 us -> 120 us (0.26)
  the two profiles are of different devices: /device:TPU:2 before, /device:TPU:1 now
where the time goes in v1:
time: 120 us; the launch traced here: 119 us
  Pallas kernels  105 us (88%)
  local copies, waits for them, and re-layouts  8.92 us (7%)
  starting transfers between devices  4.57 us (4%)
    pallas_call x1, Pallas kernels, run_exchange(): pl.pallas_call(exchange_kernel, in_specs=[pl.BlockSpec(memory_space=pltpu...  39.4 us
    pallas_call x1, Pallas kernels, run_first(): pl.pallas_call(first_kernel, grid=(STEPS,), in_specs=[smem, smem, pl.Bloc...  38.6 us
    pallas_call x1, Pallas kernels, run_last(): pl.pallas_call(last_kernel, grid=(STEPS,), in_specs=[smem, smem, pl.Block...  27 us
    ppermute x1, starting transfers between devices, on_device(): lax.ppermute(x[T - 16:], 'seq', [(k, k + 1) for k in range(NSEQ - 1)])  4.57 us
    another operation x4, local copies, waits for them, and re-layouts, by_block(): return rows.reshape(H, NC, L).transpose(1, 0, 2).reshape(NC, W)  2.9 us
  transfers between devices with their start and end apart: 1, of which 0 were waited for; matrix products, arithmetic and copies ran while one was open for 5% of the time, Pallas kernels for 0%

profile of v1, /device:TPU:1, one launch (start us, length us, event | category | flops | bytes accessed | tf_op | source)
XLA Modules:
  0.0 119.2 jit_solution(9319969313193905747)
XLA Ops:
  0.6 0.8 slice_bitcast_fusion
  1.4 4.6 %collective-permute-start = (bf16[16,1280]{1,0:T(8,128)(2,1)S(1)}, bf16[16,1280]{1,0:T(8,128)(2,1)S(1)}, u32[]{:S(2)}, u32[]{:S(2)}) collective-permute-start(bf16[16,1280]{1,0:T(8,128)(2,1)S(1)} %slice_bitcast_fusion), channel_id=1, source_target_pairs={{0,1},{1,2},{2,3},{3,4},{4,5},{5,6},{6,7},{7,8},{8,9},{9,10},{10,1... | collective-permute-start | bytes 122888 | tf_op jit(solution)/shard_map/ppermute | solution.py:514
  6.0 1.3 %broadcast_in_dim.12.cb = f32[1,1280]{1,0:T(1,128)} reshape(f32[1280]{0:T(1024)} %param.10) | data formatting | bytes 10240 | tf_op jit(solution)/shard_map/broadcast_in_dim | solution.py:516
  7.3 1.1 reshape_squeeze.7
  8.4 0.3 copy.16
  8.8 0.9 reshape.20.dtr
  9.6 1.1 reshape_squeeze.6
  10.8 0.3 copy.17
  11.1 0.9 reshape.19.ldr
  12.0 0.0 collective-permute-done.halo
  12.0 0.0 copy-start
  12.0 0.6 copy-done
  12.6 38.6 %first.1 = (bf16[4096,1280]{1,0:T(8,128)(2,1)}, f32[4096,128]{1,0:T(8,128)}, f32[8,64,128]{2,1,0:T(8,128)}, f32[8,64,128]{2,1,0:T(8,128)}, f32[16,128]{1,0:T(8,1...) custom-call(s32[128]{0:T(128)} %bitcast.26, s32[128]{0:T(128)} %bitcast.27, ...), custom_call_target="tpu_custom_call" | custom-call | tf_op jit(solution)/shard_map/first/pallas_call | solution.py:270
  51.2 39.4 %exchange.1 = (bf16[32,32,128]{2,1,0:T(8,128)(2,1)}, bf16[2,4,1056,128]{3,2,1,0:T(8,128)(2,1)}) custom-call(s32[16]{0:T(128)} %get-tuple-element.16.meta, bf16[32,32,128]{2,1,0:T(8,128)(2,1)} %bitcast.24, f32[16,128]{1,0:T(8,128)} %get-tuple-element.22.gate, bf16[2,4,1056,128]{3,2,1,0:T(8,128)(2,1)} %get-tuple-element.23.sends), custom_call_target="tpu_custom_call" | custom-call | tf_op jit(solution)/shard_map/exchange/pallas_call | solution.py:395
  90.6 27.0 %last.1 = (bf16[4096,1024]{1,0:T(8,128)(2,1)}, f32[4,2,16,64,128]{4,3,2,1,0:T(8,128)}, bf16[4,2,3,1280]{3,2,1,0:T(4,128)(2,1)}) custom-call(s32[16]{0:T(128)} %get-tuple-element.16.meta, f32[16]{0:T(128)} %skip.1, bf16[4096,1280]{1,0:T(8,128)(2,1)} %get-tuple-element.17.act, f32[4096,128]{1,0:T(8,128)} %get-tuple-element.18.cols, ...), custom_call_target="tpu_custom_call" | custom-call | tf_op jit(solution)/shard_map/last/pallas_call | solution.py:482
  117.6 1.6 %copy.13 = bf16[1,1,4,2,3,1280]{5,3,4,2,1,0:T(2,128)(2,1)} copy(bf16[1,1,4,2,3,1280]{5,4,3,2,1,0:T(4,128)(2,1)} %bitcast.25) | data formatting | bytes 122880
Async XLA Ops:
  1.4 10.6 %collective-permute-start = (bf16[16,1280]{1,0:T(8,128)(2,1)S(1)}, bf16[16,1280]{1,0:T(8,128)(2,1)S(1)}, u32[]{:S(2)}, u32[]{:S(2)}) collective-permute-start(bf16[16,1280]{1,0:T(8,128)(2,1)S(1)} %slice_bitcast_fusion), channel_id=1, source_target_pairs={{0,1},{1,2},{2,3},{3,4},{4,5},{5,6},{6,7},{7,8},{8,9},{9,10},{10,1... | collective-permute-start | bytes 122888 | tf_op jit(solution)/shard_map/ppermute | solution.py:514
  12.0 0.6 copy-start

commit v2 on v1

v2 whole, which is shorter than its diff:
```python
import functools

import jax
import jax.numpy as jnp
from jax import lax
from jax.experimental import pallas as pl
from jax.experimental.pallas import tpu as pltpu
from jax.sharding import PartitionSpec as P

MESH = pl.DeviceIdType.MESH
F32 = jnp.float32
BF16 = jnp.bfloat16
T = 4096
CH = 1280
W = 1024
H = 16
N = 128
L = 64
BLK = 256
STEPS = T // BLK
TALL = 512
NC = T // L
NSEQ = 32
NSTR = 4
PAY = 1056
BIG = 1 << 20
LOG2E = 1.4426950408889634
AT_SEND = 1
AT_SCAN = 4
AT_FIX = 8


def dot(a, b, ca=1, cb=0):
    return lax.dot_general(a, b, (((ca,), (cb,)), ((), ())), preferred_element_type=F32)


def iota(shape, dim):
    return lax.broadcasted_iota(jnp.int32, shape, dim)


def doc_start(pos, meta):
    start = jnp.full(pos.shape, meta[13], jnp.int32)
    for n in range(4):
        start = jnp.where(pos >= meta[n], meta[n], start)
    return start


def doc_end(pos, meta):
    end = jnp.full(pos.shape, T, jnp.int32)
    for n in range(3, -1, -1):
        end = jnp.where(pos < meta[n], jnp.minimum(meta[n], T), end)
    return end


def pick(table, lane):
    return jnp.take_along_axis(table, lane, axis=1)


def left(v, s):
    return pltpu.roll(v, v.shape[1] - s, 1)


def count_upto(bounds, value):
    total = bounds.shape[0]
    found = jnp.int32(0)
    step = total
    while step:
        reach = found + step
        ahead = bounds[jnp.minimum(reach, total) - 1] <= value
        found = jnp.where((reach <= total) & ahead, reach, found)
        step //= 2
    return found


def scan_docs(bounds, owners, meta, anchor):
    for k in range(16):
        meta[k] = BIG if k < 4 else 0
    total = bounds.shape[0]
    low = count_upto(bounds, anchor)
    high = jnp.minimum(count_upto(bounds, anchor + T - 1) + 1, total)
    before = jnp.where(low > 0, bounds[jnp.maximum(low - 1, 0)], 0)
    meta[13] = before - anchor

    def body(k, prev):
        bound = bounds[k]

        @pl.when((bound <= anchor + T) & (bound > prev))
        def _():
            n = meta[12]
            owner = owners[k]
            rank = jnp.int32(0)
            for m in range(4):
                same = (m < n) & (meta[4 + m] == owner)
                rank = rank + jnp.where(same, 1, 0).astype(jnp.int32)
            meta[n] = bound - anchor
            meta[4 + n] = owner
            meta[8 + n] = rank
            meta[12] = n + 1

        return bound

    lax.fori_loop(low, high, body, before)


def document_decay(meta, ld, dt, table, columns, gate):
    pos = iota((1, T), 1)
    end = doc_end(pos, meta)
    for half in range(2):
        heads = slice(8 * half, 8 * half + 8)
        v = ld[heads, :] * LOG2E
        seg = jnp.where(pos + 1 < end, left(v, 1), 0.0)
        for k in range(12):
            s = 1 << k
            seg = seg + jnp.where(pos + s < end, left(seg, s), 0.0)
        whole = jnp.exp2(v[:, :1] + seg[:, :1])
        gate[heads, :] = jnp.broadcast_to(jnp.where(meta[13] < 0, whole, 0.0), (8, N))
        weight = jnp.exp2(seg) * dt[heads, :]
        for b in range(T // TALL):
            at = b * H + 8 * half
            table[at : at + 8, :] = weight[:, b * TALL : (b + 1) * TALL]
    for b in range(TALL // N):
        columns[b * N : (b + 1) * N, :] = table[:, b * N : (b + 1) * N].T


def block_decay(meta, ld, dt, table, keys, cols, crow, grow):
    pos = iota((1, T), 1)
    place = pos % L
    base = pos - place
    ending = doc_end(pos, meta) >= base + L
    open_entry = doc_start(pos, meta) < base
    open_block = doc_start(base + (L - 1), meta) < base
    for half in range(2):
        heads = slice(8 * half, 8 * half + 8)
        v = ld[heads, :] * LOG2E
        suf = jnp.where(place + 1 < L, left(v, 1), 0.0)
        for k in range(6):
            s = 1 << k
            suf = suf + jnp.where(place + s < L, left(suf, s), 0.0)
        weight = jnp.where(ending, jnp.exp2(suf) * dt[heads, :], 0.0)
        keys[H + 8 * half : H + 8 * half + 8, :] = suf
        cum = ld[heads, :] * LOG2E
        for k in range(6):
            s = 1 << k
            cum = cum + jnp.where(place >= s, pltpu.roll(cum, s, 1), 0.0)
        entry = jnp.where(open_entry, jnp.exp2(cum), 0.0)
        for kind, value in enumerate((cum, weight, entry)):
            for b in range(2):
                at = b * 3 * H + kind * H + 8 * half
                table[at : at + 8, :] = value[:, b * (T // 2) : (b + 1) * (T // 2)]
        keys[heads, :] = cum - jnp.log2(dt[heads, :])
        suf = keys[H + 8 * half : H + 8 * half + 8, :]
        keys[H + 8 * half : H + 8 * half + 8, :] = jnp.where(open_block, jnp.exp2(cum + suf), 0.0)
    table[6 * H : N, :] = jnp.zeros((N - 6 * H, T // 2), F32)
    for b in range(T // 2 // N):
        cols[b * N : (b + 1) * N, :] = table[:, b * N : (b + 1) * N].T
    low_lane = iota((T // N, N), 1) < L
    for j in range(8):
        for row, out in ((2 * j, crow), (H + 2 * j, grow)):
            first = keys[row : row + 1, :].reshape(T // N, N)
            second = keys[row + 1 : row + 2, :].reshape(T // N, N)
            out[j, 0 : T // N, :] = jnp.where(low_lane, first, pltpu.roll(second, L, 1))
            out[j, T // N :, :] = jnp.where(low_lane, pltpu.roll(first, L, 1), second)


def block_row(c):
    return (c & 1) * (T // N) + (c >> 1)


def first_kernel(
    bounds, owners, x_ref, halo, cw, cb, ld, dt,
    act, gate, ends, sends, meta,
    xf, acc, half, table, cols, load, weights, flipped, held,
):
    i = pl.program_id(0)
    anchor = lax.axis_index("seq") * T

    @pl.when(i == 0)
    def _():
        scan_docs(bounds, owners, meta, anchor)
        document_decay(meta, ld, dt, table, cols, gate)
        acc[...] = jnp.zeros_like(acc)
        sends[...] = jnp.zeros_like(sends)
        load[...] = jnp.zeros_like(load)
        flipped[...] = jnp.zeros_like(flipped)
        held[0] = 0
        half[0:4, :] = cw[...] * 0.5
        before = iota((16, 1), 0) - 16
        real = (before >= meta[13]) & (anchor > 0)
        for j in range(CH // N):
            half[4:5, j * N : (j + 1) * N] = cb[pl.ds(j * N, N)].reshape(1, N) * 0.5
            rows = halo[:, j * N : (j + 1) * N].astype(F32)
            xf[j, 0:16, :] = jnp.where(real, rows, 0.0)

    def gather(j, lag_sum):
        lanes = slice(j * N, (j + 1) * N)
        v = half[4:5, lanes] + half[0:1, lanes] * lag_sum(0)
        for k in range(1, 4):
            v = v + half[k : k + 1, lanes] * lag_sum(k)
        return (v + v * jnp.tanh(v)).astype(BF16)

    def add_segment(j):
        for g in range(4):
            lanes = slice(g * 2 * N, (g + 1) * 2 * N)
            acc[j, :, lanes] = acc[j, :, lanes] + dot(flipped[...], load[:, lanes])

    add_segment(held[0])
    part = iota((L, N), 1) // L
    for j in range(CH // N):
        xf[j, 16 : 16 + BLK, :] = x_ref[:, j * N : (j + 1) * N].astype(F32)
        for r in range(0, BLK, L):
            lagged = lambda k: xf[j, 16 + r - k : 16 + L + r - k, :]
            act[r : r + L, j * N : (j + 1) * N] = gather(j, lagged)
            if j < 8:
                col = cols[pl.ds(pl.multiple_of((i & 1) * BLK + r, L), L), :]
                weight = pick(col, part + (2 * j + H * (i >> 1))).astype(BF16)
                weights[r : r + L, j * N : (j + 1) * N] = weight

    def fix(m, _):
        doc_begin = meta[m >> 1]
        group = (doc_begin + 2 * (m & 1)) >> 4
        again = ((m & 1) == 1) & (group == doc_begin >> 4)

        @pl.when((group >> 4 == i) & jnp.logical_not(again))
        def _():
            at = pl.multiple_of((group & 15) * 16, 16)
            pos = group * 16 + iota((16, 1), 0)
            start = doc_start(pos, meta)
            for j in range(CH // N):
                rows = xf[j, pl.ds(at, 32), :]
                lagged = lambda k: jnp.where(pos - k >= start, rows[16 - k : 32 - k], 0.0)
                act[pl.ds(at, 16), j * N : (j + 1) * N] = gather(j, lagged)

        return 0

    def take_tail(n, _):
        last = meta[n] - 1

        @pl.when(last >> 8 == i)
        def _():
            row = iota((32, 16 + BLK), 0)
            at = iota((32, 16 + BLK), 1) - 16 + i * BLK
            begin = jnp.where(n > 0, meta[jnp.maximum(n - 1, 0)], meta[13])
            total = jnp.zeros((32, N), F32)
            for j in range(CH // N):
                lag = row - 3 * j
                hit = (lag >= 0) & (lag < 3) & (at == last - 2 + lag) & (at >= begin)
                total = total + dot(jnp.where(hit, 1.0, 0.0).astype(BF16), xf[j].astype(BF16))
            sends[meta[8 + n], meta[4 + n], W:PAY, :] = total.astype(BF16)

        return 0

    touched = jnp.bool_(False)
    for n in range(4):
        touched = touched | ((meta[n] - 1) >> 8 == i) | ((meta[n] + 2) >> 8 == i)

    @pl.when(touched)
    def _():
        lax.fori_loop(0, 8, fix, 0)
        lax.fori_loop(0, 4, take_tail, 0)

    low = jnp.int32(0)
    high = jnp.int32(0)
    for n in range(4):
        low = low + jnp.where(meta[n] <= i * BLK, 1, 0).astype(jnp.int32)
        high = high + jnp.where(meta[n] <= i * BLK + BLK - 1, 1, 0).astype(jnp.int32)
    row = i * BLK + iota((BLK, 1), 0)

    def flip(j):
        begin = jnp.where(j > 0, meta[jnp.maximum(j - 1, 0)], 0)
        stop = jnp.where(j < 4, meta[jnp.minimum(j, 3)], BIG)
        kept = jnp.where((row >= begin) & (row < stop), act[:, W : W + N].astype(F32), 0.0)
        flipped[...] = kept.astype(BF16).T

    for j in range(CH // N):
        xf[j, 0:16, :] = xf[j, BLK : BLK + 16, :]
    load[...] = act[:, 0:W] * weights[...]

    def segment(j, _):
        flip(j)
        add_segment(j)
        return 0

    lax.fori_loop(low, high, segment, 0)
    flip(high)
    held[0] = high

    @pl.when(i == STEPS - 1)
    def _():
        add_segment(held[0])
        for b in range(8):
            tile = acc[meta[12], :, b * N : (b + 1) * N].T
            ends[b * N : (b + 1) * N, :] = tile.astype(BF16)

        def put(n, _):
            for b in range(8):
                tile = acc[n, :, b * N : (b + 1) * N].T
                sends[meta[8 + n], meta[4 + n], b * N : (b + 1) * N, :] = tile.astype(BF16)
            return 0

        lax.fori_loop(0, meta[12], put, 0)


def run_first(bounds, owners, x, halo, cw, cb, ld, dt):
    smem = pl.BlockSpec(memory_space=pltpu.SMEM)
    full = lambda *shape: pl.BlockSpec(shape, lambda i: (0,) * len(shape))
    return pl.pallas_call(
        first_kernel,
        grid=(STEPS,),
        in_specs=[
            smem, smem, pl.BlockSpec((BLK, CH), lambda i: (i, 0)), full(16, CH), full(4, CH),
            full(CH), full(H, T), full(H, T),
        ],
        out_specs=[
            pl.BlockSpec((BLK, CH), lambda i: (i, 0)), full(H, N), full(W, N), full(2, NSTR, PAY, N), smem,
        ],
        out_shape=[
            jax.ShapeDtypeStruct((T, CH), BF16),
            jax.ShapeDtypeStruct((H, N), F32), jax.ShapeDtypeStruct((W, N), BF16),
            jax.ShapeDtypeStruct((2, NSTR, PAY, N), BF16), jax.ShapeDtypeStruct((16,), jnp.int32),
        ],
        scratch_shapes=[
            pltpu.VMEM((CH // N, BLK + 16, N), F32), pltpu.VMEM((5, N, W), F32),
            pltpu.VMEM((8, CH), F32), pltpu.VMEM((N, TALL), F32), pltpu.VMEM((TALL, N), F32),
            pltpu.VMEM((BLK, W), BF16),
            pltpu.VMEM((BLK, W), BF16), pltpu.VMEM((N, BLK), BF16), pltpu.SMEM((1,), jnp.int32),
        ],
        compiler_params=pltpu.CompilerParams(dimension_semantics=("arbitrary",)),
        name="first",
    )(bounds, owners, x, halo, cw, cb, ld, dt)


def middle_kernel(
    meta, skip, act, ld, dt, ends, gate, sends,
    out, cols, grow, carried_out, got,
    h, hb, skips, crow, table, keys, seen, seen_gate, prefix, carried, fixed, my_gate,
    s1, r1, s2, r2, s3, r3, s4, r4, own_sem,
):
    i = pl.program_id(0)
    me = lax.axis_index("seq")
    st = lax.axis_index("stream")

    def handoff(k, slot, src, s, r):
        to = lax.rem(st + k, NSTR)
        return pltpu.make_async_remote_copy(
            src_ref=src.at[to], dst_ref=got.at[slot, st], send_sem=s.at[k], recv_sem=r.at[k],
            device_id=(to, me), device_id_type=MESH,
        )

    def spread(k):
        to = lax.rem(me + k, NSEQ)
        state = pltpu.make_async_remote_copy(
            src_ref=ends.at[to], dst_ref=seen.at[me], send_sem=s1.at[k], recv_sem=r1.at[k],
            device_id=(st, to), device_id_type=MESH,
        )
        factor = pltpu.make_async_remote_copy(
            src_ref=my_gate.at[pl.ds(lax.div(to, 2), 1)], dst_ref=seen_gate.at[pl.ds(me, 1)],
            send_sem=s2.at[k], recv_sem=r2.at[k], device_id=(st, to), device_id_type=MESH,
        )
        return state, factor

    def give(k):
        to = lax.rem(me + k, NSEQ)
        return pltpu.make_async_remote_copy(
            src_ref=prefix.at[to], dst_ref=carried.at[me], send_sem=s1.at[NSEQ + k],
            recv_sem=r1.at[NSEQ + k], device_id=(st, to), device_id_type=MESH,
        )

    def keep_own(slot, src):
        return pltpu.make_async_copy(src.at[st], got.at[slot, st], own_sem.at[slot])

    @pl.when(i == 0)
    def _():
        barrier = pltpu.get_barrier_semaphore()

        @pl.loop(1, NSEQ)
        def _(k):
            pl.semaphore_signal(
                barrier, inc=1, device_id=(st, lax.rem(me + k, NSEQ)), device_id_type=MESH
            )

        for k in range(1, NSTR):
            pl.semaphore_signal(
                barrier, inc=1, device_id=(lax.rem(st + k, NSTR), me), device_id_type=MESH
            )
        my_gate[...] = jnp.where(meta[12] == 0, gate[...], 0.0)
        block_decay(meta, ld, dt, table, keys, cols, crow, grow)
        h[...] = jnp.zeros_like(h)
        hb[...] = jnp.zeros_like(hb)
        lane = iota((L, N), 1)
        for j in range(8):
            gain = jnp.where(lane < L, skip[2 * j], skip[2 * j + 1])
            skips[j] = jnp.where(lane % L == iota((L, N), 0), gain, 0.0).astype(BF16)

    @pl.when(i == AT_SEND)
    def _():
        pl.semaphore_wait(pltpu.get_barrier_semaphore(), NSEQ - 1 + NSTR - 1)

        @pl.loop(1, NSEQ)
        def _(k):
            state, factor = spread(k)
            factor.start()
            state.start()

        for k in range(1, NSTR):
            handoff(k, 1, sends.at[1], s3, r3).start()
        keep_own(1, sends.at[1]).start()
        seen[pl.ds(me, 1)] = ends[pl.ds(me, 1)]
        seen_gate[pl.ds(me, 1), :] = my_gate[pl.ds(lax.div(me, 2), 1), :]

    @pl.when(i == AT_SCAN)
    def _():
        @pl.loop(1, NSEQ)
        def _(k):
            state, factor = spread(k)
            factor.wait()
            state.wait()

        def step(q, state):
            prefix[q] = state.astype(BF16)
            return seen[q].astype(F32) + seen_gate[pl.ds(q, 1), :] * state

        lax.fori_loop(0, NSEQ, step, jnp.zeros((32, N), F32), unroll=8)

        @pl.loop(1, NSEQ)
        def _(k):
            give(k).start()

        carried[pl.ds(me, 1)] = prefix[pl.ds(me, 1)]

    @pl.when(i == AT_FIX)
    def _():
        @pl.loop(1, NSEQ)
        def _(k):
            give(k).wait()

        def correct(d, _):
            lift = jnp.where(meta[12] > 0, gate[pl.ds(lax.div(d, 2), 1), :], 0.0)
            extra = carried[d].astype(F32) * lift
            rows = pl.ds(pl.multiple_of(d * 32, 32), 32)
            for o in range(NSTR):
                mine = jnp.where(meta[4] == o, extra, 0.0)
                fixed[o, rows, :] = (sends[0, o, rows, :].astype(F32) + mine).astype(BF16)
            return 0

        lax.fori_loop(0, NSEQ, correct, 0, unroll=8)
        for o in range(NSTR):
            fixed[o, W:PAY, :] = sends[0, o, W:PAY, :]
        for k in range(1, NSTR):
            handoff(k, 0, fixed, s4, r4).start()
        keep_own(0, fixed).start()
        carried_out[...] = carried[...]

    part = iota((L, N), 1) // L
    lane = part + 3 * H * (i >> 3)
    zero = jnp.zeros((L, N), BF16)
    for q in range(BLK // L):
        rows = slice(q * L, (q + 1) * L)
        c = i * (BLK // L) + q
        cmat = act[rows, W + N : CH]
        bmat = act[rows, W : W + N]
        flipped = bmat.T
        at = (i & (STEPS // 2 - 1)) * BLK + q * L
        col = cols[pl.ds(pl.multiple_of(at, L), L), :]
        score = dot(cmat, jnp.concatenate([bmat, bmat], 0), 1, 1)
        pos = c * L + iota((L, N), 0)
        src = c * L + iota((L, N), 1) % L
        keep = (src <= pos) & (src >= doc_start(pos, meta))
        score = jnp.where(keep, score, 0.0).astype(BF16)
        for g in range(4):
            wide = slice(g * 2 * N, (g + 1) * 2 * N)
            mix, pairs, entry, loads = [], [], [], []
            for j in (2 * g, 2 * g + 1):
                x = act[rows, j * N : (j + 1) * N]
                spread = pick(col, lane + 2 * j) - crow[j, pl.ds(block_row(c), 1), :]
                mix.append(jnp.exp2(jnp.minimum(spread, 30.0)).astype(BF16) * score + skips[j])
                for half in (0, 1):
                    own = jnp.where(part == half, x, zero)
                    pairs.append(jnp.concatenate([own, zero] if j == 2 * g else [zero, own], 1))
                loads.append(x * pick(col, lane + (2 * j + H)).astype(BF16))
                entry.append(pick(col, lane + (2 * j + 2 * H)))
            inner = dot(jnp.concatenate(mix, 1), jnp.concatenate(pairs, 0))
            outer = dot(cmat, hb[:, wide]) * jnp.concatenate(entry, 1)
            out[rows, wide] = (inner + outer).astype(BF16)
            fresh = dot(flipped, jnp.concatenate(loads, 1))
            for j in (0, 1):
                lanes = slice((2 * g + j) * N, (2 * g + j + 1) * N)
                state = grow[2 * g + j, pl.ds(block_row(c), 1), :] * h[:, lanes] + fresh[:, j * N : (j + 1) * N]
                h[:, lanes] = state
                hb[:, lanes] = state.astype(BF16)

    @pl.when(i == STEPS - 1)
    def _():
        keep_own(1, sends.at[1]).wait()
        keep_own(0, fixed).wait()
        for k in range(1, NSTR):
            handoff(k, 1, sends.at[1], s3, r3).wait()
            handoff(k, 0, fixed, s4, r4).wait()


def run_middle(meta, skip, act, ld, dt, ends, gate, sends):
    smem = pl.BlockSpec(memory_space=pltpu.SMEM)
    full = lambda *shape: pl.BlockSpec(shape, lambda i: (0,) * len(shape))
    dma = pltpu.SemaphoreType.DMA
    return pl.pallas_call(
        middle_kernel,
        grid=(STEPS,),
        in_specs=[
            smem, smem, pl.BlockSpec((BLK, CH), lambda i: (i, 0)),
            full(H, T), full(H, T),
            full(NSEQ, 32, N), full(H, N), full(2, NSTR, PAY, N),
        ],
        out_specs=[
            pl.BlockSpec((BLK, W), lambda i: (i, 0)), full(T // 2, N), full(8, NC, N),
            full(NSEQ, 32, N), pl.BlockSpec(memory_space=pl.ANY),
        ],
        out_shape=[
            jax.ShapeDtypeStruct((T, W), BF16), jax.ShapeDtypeStruct((T // 2, N), F32),
            jax.ShapeDtypeStruct((8, NC, N), F32),
            jax.ShapeDtypeStruct((NSEQ, 32, N), BF16),
            jax.ShapeDtypeStruct((2, NSTR, PAY, N), BF16),
        ],
        scratch_shapes=[
            pltpu.VMEM((N, W), F32), pltpu.VMEM((N, W), BF16), pltpu.VMEM((8, L, N), BF16),
            pltpu.VMEM((8, NC, N), F32), pltpu.VMEM((N, T // 2), F32), pltpu.VMEM((2 * H, T), F32),
            pltpu.VMEM((NSEQ, 32, N), BF16), pltpu.VMEM((NSEQ, N), F32),
            pltpu.VMEM((NSEQ, 32, N), BF16), pltpu.VMEM((NSEQ, 32, N), BF16),
            pltpu.VMEM((NSTR, PAY, N), BF16), pltpu.VMEM((H, N), F32),
            dma((2 * NSEQ,)), dma((2 * NSEQ,)), dma((NSEQ,)), dma((NSEQ,)),
            dma((NSTR,)), dma((NSTR,)), dma((NSTR,)), dma((NSTR,)), dma((2,)),
        ],
        compiler_params=pltpu.CompilerParams(
            collective_id=0, has_side_effects=True, dimension_semantics=("arbitrary",)
        ),
        name="middle",
    )(meta, skip, act, ld, dt, ends, gate, sends)


def last_kernel(meta, partial, cmats, cols, grow, carried, got, out, ssm, tails, turned, through):
    i = pl.program_id(0)

    @pl.when(i == 0)
    def _():
        through[...] = jnp.ones_like(through)
        for j in range(8):
            turned[:, j * N : (j + 1) * N] = carried[j * N : (j + 1) * N, :].T

    @pl.when(i < 2 * NSTR)
    def _():
        ssm[...] = got[0, 0, 0:W, :].astype(F32).reshape(ssm.shape)
        tail = got[0, 0, W:PAY, :].astype(F32)
        for j in range(CH // N):
            for k in range(3):
                row = tail[3 * j + k : 3 * j + k + 1, :].astype(BF16)
                tails[0, 0, k : k + 1, j * N : (j + 1) * N] = row

    inside = (meta[13] < 0) & (i * TALL < meta[0])

    @pl.when(jnp.logical_not(inside))
    def _():
        out[...] = partial[...]

    @pl.when(inside)
    def _():
        part = iota((TALL, N), 1) // L + 3 * H * (i // (T // 2 // TALL))
        for j in range(8):
            lanes = slice(j * N, (j + 1) * N)
            if j % 2 == 0:
                extra = dot(cmats[...], turned[:, j * N : (j + 2) * N])
            here = through[j]
            for q in range(TALL // L):
                rows = slice(q * L, (q + 1) * L)
                factor = pick(cols[rows, :], part[rows] + (2 * j + 2 * H)) * here
                half = extra[rows, (j % 2) * N : (j % 2 + 1) * N]
                out[rows, lanes] = (partial[rows, lanes].astype(F32) + factor * half).astype(BF16)
                here = here * grow[j, pl.ds(block_row(i * (TALL // L) + q), 1), :]
            through[j] = here


def run_last(meta, partial, act, cols, grow, carried, got):
    smem = pl.BlockSpec(memory_space=pltpu.SMEM)
    full = lambda *shape: pl.BlockSpec(shape, lambda i: (0,) * len(shape))
    slot = lambda i: jnp.minimum(i, 7)
    return pl.pallas_call(
        last_kernel,
        grid=(T // TALL,),
        in_specs=[
            smem, pl.BlockSpec((TALL, W), lambda i: (i, 0)),
            pl.BlockSpec((TALL, N), lambda i: (i, CH // N - 1)),
            pl.BlockSpec((TALL, N), lambda i: (i % (T // 2 // TALL), 0)), full(8, NC, N), full(W, N),
            pl.BlockSpec((1, 1, PAY, N), lambda i: (slot(i) % 2, slot(i) // 2, 0, 0)),
        ],
        out_specs=[
            pl.BlockSpec((TALL, W), lambda i: (i, 0)),
            pl.BlockSpec((1, 1, H, L, N), lambda i: (slot(i) // 2, slot(i) % 2, 0, 0, 0)),
            pl.BlockSpec((1, 1, 3, CH), lambda i: (slot(i) // 2, slot(i) % 2, 0, 0)),
        ],
        out_shape=[
            jax.ShapeDtypeStruct((T, W), BF16),
            jax.ShapeDtypeStruct((NSTR, 2, H, L, N), F32),
            jax.ShapeDtypeStruct((NSTR, 2, 3, CH), BF16),
        ],
        scratch_shapes=[pltpu.VMEM((N, W), BF16), pltpu.VMEM((8, 1, N), F32)],
        compiler_params=pltpu.CompilerParams(dimension_semantics=("arbitrary",)),
        name="last",
    )(meta, partial, act, cols, grow, carried, got)


def on_device(x, cw, cb, dt, ld, skip, bounds, owners):
    x, dt, ld = x[0], dt[0], ld[0]
    halo = lax.ppermute(x[T - 16 :], "seq", [(k, k + 1) for k in range(NSEQ - 1)])
    act, gate, ends, sends, meta = run_first(
        bounds[0], owners[0], x, halo, cw, cb, ld, dt
    )
    partial, cols, grow, carried, got = run_middle(
        meta, skip, act, ld, dt, ends.reshape(NSEQ, 32, N), gate, sends
    )
    out, ssm, tails = run_last(meta, partial, act, cols, grow, carried.reshape(W, N), got)
    return out[None], ssm[None, None], tails[None, None]


def solution(mesh):
    in_specs = (
        P("stream", "seq", None),
        P(),
        P(),
        P("stream", None, "seq"),
        P("stream", None, "seq"),
        P(),
        P("stream", None),
        P("stream", None),
    )
    out_specs = (
        P("stream", "seq", None),
        P("stream", "seq", None, None, None, None, None),
        P("stream", "seq", None, None, None, None),
    )
    return jax.shard_map(
        on_device, mesh=mesh, in_specs=in_specs, out_specs=out_specs, check_vma=False
    )
```

time: 120 us -> 92.8 us (0.77)
  Pallas kernels: 105 us -> 82.2 us
  local copies, waits for them, and re-layouts: 8.92 us -> 2.97 us
    pallas_call x1, Pallas kernels: 38.6 us -> 26.7 us  [run_first(): pl.pallas_call(first_kernel, grid=(STEPS,), in_specs=[smem, smem, pl.Bloc...]
    pallas_call x2, Pallas kernels: 66.4 us -> 55.5 us  [the longest x1 41.9 us: run_middle(): pl.pallas_call(middle_kernel, grid=(STEPS,), in_specs=[smem, smem, pl.Blo...]
    another operation x4 -> x0, local copies, waits for them, and re-layouts: 2.9 us -> none  [by_block(): return rows.reshape(H, NC, L).transpose(1, 0, 2).reshape(NC, W)]
    reshape x2 -> x0, local copies, waits for them, and re-layouts: 1.76 us -> none  [by_block(): return rows.reshape(H, NC, L).transpose(1, 0, 2).reshape(NC, W)]
    broadcast_in_dim x1 -> x0, local copies, waits for them, and re-layouts: 1.3 us -> none  [on_device(): cb[None]]
  transfers between devices with their start and end apart: 1 -> 1, of which waited for: 0 -> 1; matrix products, arithmetic and copies ran while one was open for 5% -> 0% of each run, Pallas kernels for 0% -> 0%
where the time goes in v2:
time: 92.8 us; the launch traced here: 91.5 us
  Pallas kernels  82.2 us (89%)
  starting transfers between devices  4.57 us (5%)
  local copies, waits for them, and re-layouts  2.97 us (3%)
  waiting for transfers between devices  1.08 us (1%)
    pallas_call x1, Pallas kernels, run_middle(): pl.pallas_call(middle_kernel, grid=(STEPS,), in_specs=[smem, smem, pl.Blo...  41.9 us
    pallas_call x1, Pallas kernels, run_first(): pl.pallas_call(first_kernel, grid=(STEPS,), in_specs=[smem, smem, pl.Bloc...  26.7 us
    pallas_call x1, Pallas kernels, run_last(): pl.pallas_call(last_kernel, grid=(T // TALL,), in_specs=[smem, pl.BlockSp...  13.7 us
    ppermute x1, starting transfers between devices, on_device(): lax.ppermute(x[T - 16:], 'seq', [(k, k + 1) for k in range(NSEQ - 1)])  4.57 us
    unnamed x3, local copies, waits for them, and re-layouts  2.18 us
  transfers between devices with their start and end apart: 1, of which 1 were waited for; matrix products, arithmetic and copies ran while one was open for 0% of the time, Pallas kernels for 0%

profile of v2, /device:TPU:1, one launch (start us, length us, event | category | flops | bytes accessed | tf_op | source)
XLA Modules:
  0.0 91.5 jit_solution(9164957566534508270)
XLA Ops:
  0.6 0.8 slice_bitcast_fusion
  1.4 4.6 %collective-permute-start = (bf16[16,1280]{1,0:T(8,128)(2,1)S(1)}, bf16[16,1280]{1,0:T(8,128)(2,1)S(1)}, u32[]{:S(2)}, u32[]{:S(2)}) collective-permute-start(bf16[16,1280]{1,0:T(8,128)(2,1)S(1)} %slice_bitcast_fusion), channel_id=1, source_target_pairs={{0,1},{1,2},{2,3},{3,4},{4,5},{5,6},{6,7},{7,8},{8,9},{9,10},{10,1... | collective-permute-start | bytes 122888 | tf_op jit(solution)/shard_map/ppermute | solution.py:610
  6.0 1.1 %collective-permute-done.halo = bf16[16,1280]{1,0:T(8,128)(2,1)S(1)} collective-permute-done((bf16[16,1280]{1,0:T(8,128)(2,1)S(1)}, bf16[16,1280]{1,0:T(8,128)(2,1)S(1)}, u32[]{:S(2)}, u32[]{:S(2)}) %collective-permute-start) | collective-permute-done | bytes 40992 | tf_op jit(solution)/shard_map/ppermute | solution.py:610
  7.1 0.0 copy-start
  7.1 0.6 copy-done
  7.7 26.7 %first.1 = (bf16[4096,1280]{1,0:T(8,128)(2,1)}, f32[16,128]{1,0:T(8,128)}, bf16[1024,128]{1,0:T(8,128)(2,1)}, bf16[2,4,1056,128]{3,2,1,0:T(8,128)(2,1)}, s32[16]{0:T(128)}) custom-call(s32[128]{0:T(128)} %bitcast.20, s32[128]{0:T(128)} %bitcast.21, bf16[4096,1280]{1,0:T(8,128)(2,1)} %bitcast.12, bf16[16,1280]{1,0:T(8,128)(2,1)} %copy-done, f32[4,1280]{1,0:T(4,128)} %cw.1, ...), custom_call_target="tpu_custom_call" | custom-call | tf_op jit(solution)/shard_map/first/pallas_call | solution.py:306
  34.4 41.9 %middle.1 = (bf16[4096,1024]{1,0:T(8,128)(2,1)}, f32[2048,128]{1,0:T(8,128)}, f32[8,64,128]{2,1,0:T(8,128)}, bf16[32,32,128]{2,1,0:T(8,128)(2,1)}, bf16[2,4,1056,128]{3,2,1,0:T(8,128)(2,1)}) custom-call(s32[16]{0:T(128)} %get-tuple-element.16.meta, f32[16]{0:T(128)} %skip.1, bf16[4096,1280]{1,0:T(8,128)(2,1)} %get-tuple-element.17.act.cmats, ...), custom_call_target="tpu_custom_call" | custom-call | tf_op jit(solution)/shard_map/middle/pallas_call | solution.py:504
  76.3 13.7 %last.1 = (bf16[4096,1024]{1,0:T(8,128)(2,1)}, f32[4,2,16,64,128]{4,3,2,1,0:T(8,128)}, bf16[4,2,3,1280]{3,2,1,0:T(4,128)(2,1)}) custom-call(s32[16]{0:T(128)} %get-tuple-element.16.meta, bf16[4096,1024]{1,0:T(8,128)(2,1)} %get-tuple-element.21.partial, bf16[4096,1280]{1,0:T(8,128)(2,1)} %get-tuple-element.17.act.cmats, f32[2048,128]{1,0:T(8,128)} %get-tuple-element.22.cols, ...), custom_call_target="tpu_custom_call" | custom-call | tf_op jit(solution)/shard_map/last/pallas_call | solution.py:583
  90.0 1.6 %copy.11 = bf16[1,1,4,2,3,1280]{5,3,4,2,1,0:T(2,128)(2,1)} copy(bf16[1,1,4,2,3,1280]{5,4,3,2,1,0:T(4,128)(2,1)} %bitcast.19) | data formatting | bytes 122880
Async XLA Ops:
  1.4 5.7 %collective-permute-start = (bf16[16,1280]{1,0:T(8,128)(2,1)S(1)}, bf16[16,1280]{1,0:T(8,128)(2,1)S(1)}, u32[]{:S(2)}, u32[]{:S(2)}) collective-permute-start(bf16[16,1280]{1,0:T(8,128)(2,1)S(1)} %slice_bitcast_fusion), channel_id=1, source_target_pairs={{0,1},{1,2},{2,3},{3,4},{4,5},{5,6},{6,7},{7,8},{8,9},{9,10},{10,1... | collective-permute-start | bytes 122888 | tf_op jit(solution)/shard_map/ppermute | solution.py:610
  7.1 0.6 copy-start
